TPU v7x, 256 devices: a whole 4x4x8 slice. The times are simulated.
256 devices in a mesh: cg: 16 (over z, x_lo), vg: 16 (over x_hi, y, core).
Axes of the slice: x: 4 (x_hi: 2, x_lo: 2; x = x_hi * 2 + x_lo), y: 4, z: 8, core: 2. Of those that a mesh axis runs over, the one named last changes fastest.
Arguments:
- con_embed: float32 [262144, 128], P(('cg', 'vg')), may hold values from -6 to 6
- var_embed: float32 [262144, 128], P(('vg', 'cg')), may hold values from -6 to 6
- row_coef: float32 [262144], P(('cg', 'vg')), may hold values from 0.3 to 3
- col_coef: float32 [262144], P(('vg', 'cg')), may hold values from 0.3 to 3
- self_weight: float32 [128, 128], replicated, may hold values from -0.5 to 0.5
- msg_weight: float32 [128, 128], replicated, may hold values from -0.0234375 to 0.0234375
- timestep: int32 [1], replicated, may hold values from 0 to 999
- tile_rows: int32 [16, 16, 16], P('cg', 'vg'), may hold values from 0 to 31, as said below
- tile_cols: int32 [16, 16, 16], P('cg', 'vg'), may hold values from 0 to 31, as said below
- pattern: bfloat16 [16, 16, 16, 512, 512], P('cg', 'vg'), may hold values from -6 to 6
- cotangent: float32 [262144, 128], P(('cg', 'vg')), may hold values from -6 to 6
Outputs:
- con_update: float32 [262144, 128], P(('cg', 'vg'))
- grad_con: float32 [262144, 128], P(('cg', 'vg'))
- grad_var: float32 [262144, 128], P(('vg', 'cg'))
- grad_msg: float32 [128, 128], replicated
- grad_self: float32 [128, 128], replicated
Inputs may be any that keep to these rules, and one draw needn't show every extreme that they name: `tile_rows`: every device lists tile row 0 and tile row 31; a device lists distinct tiles unless 16 exceeds 32 * 32, and repeated tiles add. `tile_cols`: every device lists tile column 0 and tile column 31, together with the rows above: tiles (0, 0) and (31, 31) are on every list.
All inputs are finite; a program needn't handle non-finite values.
Results may differ from a plain program's by a relative error of at most 0.007.
Values may be sent and summed in bfloat16 or wider, within the bound.
No kernel may reach another device: no remote copies, remote signals or barrier semaphores. Data moves between devices by JAX's collectives and lax.ppermute only.
A program may use at most 128 MiB of HBM per device.

v0:
```python
import math
import jax
import jax.numpy as jnp
from jax import lax
from jax.sharding import PartitionSpec as P

H = 128
TB = 512


def body(
    con_embed,
    var_embed,
    row_coef,
    col_coef,
    self_weight,
    msg_weight,
    timestep,
    tile_rows,
    tile_cols,
    pattern,
    cotangent,
):
    highest = lax.Precision.HIGHEST
    con_count = con_embed.shape[0]
    var_count = var_embed.shape[0]
    row_blocks = con_count * lax.axis_size("vg") // TB
    col_blocks = var_count * lax.axis_size("cg") // TB
    row_index = tile_rows.reshape(-1)
    col_index = tile_cols.reshape(-1)
    tile_count = row_index.shape[0]
    per_turn = math.gcd(tile_count, 8)
    turns = tile_count // per_turn
    patterns_here = pattern.reshape(turns, per_turn, TB, TB)
    row_turns = row_index.reshape(turns, per_turn)
    col_turns = col_index.reshape(turns, per_turn)
    gathered, scales = (
        lax.all_gather(var_embed, "cg", axis=0, tiled=True),
        lax.all_gather(col_coef, "cg", axis=0, tiled=True),
    )
    projected = (
        jnp.dot(gathered, msg_weight, precision=highest, preferred_element_type=jnp.float32)
        * scales[:, None]
    ).astype(jnp.bfloat16)
    source_blocks = projected.reshape(col_blocks, TB, H)
    row_ids = jnp.arange(row_blocks, dtype=jnp.int32)
    col_ids = jnp.arange(col_blocks, dtype=jnp.int32)

    def forward_turn(running, inputs):
        rows_now, cols_now, tile_mask = inputs
        products = jnp.einsum(
            "grc,gch->grh", tile_mask, source_blocks[cols_now], preferred_element_type=jnp.float32
        )
        selector = (rows_now[None, :] == row_ids[:, None]).astype(jnp.float32)
        running = running + jnp.dot(
            selector,
            products.reshape(per_turn, TB * H),
            precision=highest,
            preferred_element_type=jnp.float32,
        )
        return (running, None)

    forward_sum, _ = lax.scan(
        forward_turn,
        jnp.zeros((row_blocks, TB * H), jnp.float32),
        (row_turns, col_turns, patterns_here),
    )
    messages = lax.psum_scatter(
        forward_sum.reshape(row_blocks * TB, H), "vg", scatter_dimension=0, tiled=True
    )
    frequency = jnp.exp(-math.log(10000.0) * jnp.arange(H // 2, dtype=jnp.float32) / (H // 2))
    phases = timestep[0].astype(jnp.float32) * frequency
    time_embed = jnp.concatenate([jnp.sin(phases), jnp.cos(phases)])
    preact = (
        jnp.dot(con_embed, self_weight, precision=highest, preferred_element_type=jnp.float32)
        + row_coef[:, None] * messages
        + time_embed[None, :]
    )
    sigmoid_z = jax.nn.sigmoid(preact)
    con_update = con_embed + preact * sigmoid_z
    grad_pre = cotangent * sigmoid_z * (1.0 + preact * (1.0 - sigmoid_z))
    grad_con = cotangent + jnp.dot(
        grad_pre, self_weight.T, precision=highest, preferred_element_type=jnp.float32
    )
    local_self = jnp.dot(
        con_embed.T, grad_pre, precision=highest, preferred_element_type=jnp.float32
    )
    grad_messages = (row_coef[:, None] * grad_pre).astype(jnp.bfloat16)
    whole_rows = lax.all_gather(grad_messages, "vg", axis=0, tiled=True).reshape(row_blocks, TB, H)

    def backward_turn(running, inputs):
        rows_now, cols_now, tile_mask = inputs
        products = jnp.einsum(
            "grc,grh->gch", tile_mask, whole_rows[rows_now], preferred_element_type=jnp.float32
        )
        selector = (cols_now[None, :] == col_ids[:, None]).astype(jnp.float32)
        running = running + jnp.dot(
            selector,
            products.reshape(per_turn, TB * H),
            precision=highest,
            preferred_element_type=jnp.float32,
        )
        return (running, None)

    backward_sum, _ = lax.scan(
        backward_turn,
        jnp.zeros((col_blocks, TB * H), jnp.float32),
        (row_turns, col_turns, patterns_here),
    )
    grad_projected = lax.psum_scatter(
        backward_sum.reshape(col_blocks * TB, H), "cg", scatter_dimension=0, tiled=True
    )
    grad_lin = col_coef[:, None] * grad_projected
    grad_var = jnp.dot(
        grad_lin, msg_weight.T, precision=highest, preferred_element_type=jnp.float32
    )
    local_msg = jnp.dot(
        var_embed.T, grad_lin, precision=highest, preferred_element_type=jnp.float32
    )
    grad_msg, grad_self = lax.psum((local_msg, local_self), ("cg", "vg"))
    return (con_update, grad_con, grad_var, grad_msg, grad_self)


def solution(mesh):
    in_specs = (
        P(("cg", "vg"), None),
        P(("vg", "cg"), None),
        P(("cg", "vg")),
        P(("vg", "cg")),
        P(),
        P(),
        P(),
        P("cg", "vg", None),
        P("cg", "vg", None),
        P("cg", "vg", None, None, None),
        P(("cg", "vg"), None),
    )
    out_specs = (P(("cg", "vg"), None), P(("cg", "vg"), None), P(("vg", "cg"), None), P(), P())
    return jax.shard_map(body, mesh=mesh, in_specs=in_specs, out_specs=out_specs, check_vma=False)
```

profile of v0, /device:TPU:2, one launch (start us, length us, event | category | flops | bytes accessed | tf_op | source)
XLA Modules:
  0.0 902.7 jit_solution(3706184754790364743)
XLA Ops:
  11.3 37.0 %all_gather.10 = f32[16384]{0:T(1024)S(1)} all-gather(f32[1024]{0:T(1024)} %param.18), channel_id=1, replica_groups=mesh['cg'=16,'vg'=16] {'cg'}, dimensions={0}, use_global_device_ids=true | all-gather | bytes 69632 | tf_op jit(solution)/shard_map/all_gather | solution.py:39
  48.3 146.8 %all-gather.3.cloned.1.call-done = f32[16384,128]{1,0:T(8,128)} async-done(((f32[1024,128]{1,0:T(8,128)}), f32[16384,128]{1,0:T(8,128)}) %all-gather.3.cloned.1.call-update) | async-done | bytes 8388624 | tf_op jit(solution)/shard_map/all_gather | solution.py:38
  195.1 18.7 %fusion.30 = bf16[16384,128]{1,0:T(8,128)(2,1)} fusion(f32[16384,128]{1,0:T(8,128)} %all-gather.3.cloned.1.call-done, f32[128,128]{1,0:T(8,128)S(1)} %copy-done, f32[16384]{0:T(1024)S(1)} %all_gather.10), kind=kOutput, calls=%fused_computation.39 | convolution fusion | flops 3225419776 | bytes 12713984 | tf_op jit(solution)/shard_map/dot_general | solution.py:42
  213.8 30.1 %while.22 = (s32[]{:T(128)}, f32[32,65536]{1,0:T(8,128)}, s32[2,8]{1,0:T(2,128)S(1)}, bf16[2,8,512,512]{3,2,1,0:T(8,128)(2,1)}, s32[2,8]{1,0:T(2,128)S(1)}, /*in...) while((s32[]{:T(128)}, f32[32,65536]{1,0:T(8,128)}, s32[2,8]{1,0:T(2,128)S(1)}, ...), condition=%wide.region_1.2_spmd.clone, body=%wide.region_0.1_spmd.clone.sunk | while | flops 742393088 | bytes 28316484 | solution.py:63
  213.8 2.9 gather_fusion
  216.7 3.4 fusion.65
  220.2 7.5 convolution_add_fusion.6
  227.7 2.9 gather_fusion
  230.7 3.4 fusion.65
  234.1 9.7 %convolution_add_fusion.6 = f32[32,65536]{1,0:T(8,128)} fusion(f32[32,65536]{1,0:T(8,128)} %get-tuple-element.263, pred[]{:T(512)S(6)} %compare.6, f32[1,8,512,128]{3,2,1,0:T(8,128)S(1)} %fusion.65, s32[8]{0:T(128)S(1)} %fusion.66), kind=kOutput, calls=%fused_computation.4.clone.1 | convolution fusion | flops 205521152 | bytes 18874400 | tf_op jit(solution)/shard_map/while/body/eval_jaxpr/dot_general | solution.py:55
  243.8 7.3 reshape.96
  252.1 110.5 %reduce-scatter.3.cloned.1.call-done = f32[1024,128]{1,0:T(8,128)} async-done(((f32[16384,128]{1,0:T(8,128)}), f32[1024,128]{1,0:T(8,128)}) %reduce-scatter.3.cloned.1.call-update) | async-done | bytes 524304 | tf_op jit(solution)/shard_map/reduce_scatter | solution.py:68
  365.7 12.4 %copy.20 = bf16[1,1,16,512,512]{3,4,2,1,0:T(8,128)(2,1)} copy(bf16[1,1,16,512,512]{4,3,2,1,0:T(8,128)(2,1)} %bitcast.88) | data formatting | bytes 16777216 | tf_op args[9]
  378.0 47.1 %all-gather.5.cloned.1.call-done = bf16[16384,128]{1,0:T(8,128)(2,1)} async-done(((bf16[1024,128]{1,0:T(8,128)(2,1)}), bf16[16384,128]{1,0:T(8,128)(2,1)}) %all-gather.5.cloned.1.call-update) | async-done | bytes 4194320 | tf_op jit(solution)/shard_map/all_gather | solution.py:89
  425.2 29.9 %while.23 = (s32[]{:T(128)}, f32[32,65536]{1,0:T(8,128)}, s32[2,8]{1,0:T(2,128)S(1)}, bf16[2,8,512,512]{2,3,1,0:T(8,128)(2,1)}, s32[2,8]{1,0:T(2,128)S(1)}, /*in...) while((s32[]{:T(128)}, f32[32,65536]{1,0:T(8,128)}, s32[2,8]{1,0:T(2,128)S(1)}, ...), condition=%wide.region_4.5_spmd.clone, body=%wide.region_3.4_spmd.clone.sunk | while | flops 742393088 | bytes 28316484 | solution.py:105
  425.2 2.9 gather_fusion.1
  428.1 3.4 fusion.71
  431.6 7.4 convolution_add_fusion.7
  439.0 2.9 gather_fusion.1
  442.0 3.4 fusion.71
  445.4 9.6 %convolution_add_fusion.7 = f32[32,65536]{1,0:T(8,128)} fusion(f32[32,65536]{1,0:T(8,128)} %get-tuple-element.287, pred[]{:T(512)S(6)} %compare.7, f32[1,8,512,128]{3,2,1,0:T(8,128)S(1)} %fusion.71, s32[8]{0:T(128)S(1)} %fusion.72), kind=kOutput, calls=%fused_computation.21.clone.1 | convolution fusion | flops 205521152 | bytes 18874400 | tf_op jit(solution)/shard_map/while/body/eval_jaxpr/dot_general | solution.py:97
  455.0 7.4 reshape.98
  467.1 175.9 %reduce-scatter.5.cloned.1.call-done = f32[1024,128]{1,0:T(8,128)} async-done(((f32[16384,128]{1,0:T(8,128)}), f32[1024,128]{1,0:T(8,128)}) %reduce-scatter.5.cloned.1.call-update) | async-done | bytes 524304 | tf_op jit(solution)/shard_map/reduce_scatter | solution.py:110
  648.3 244.7 %all-reduce.3.cloned.1.call-done = (f32[128,128]{0,1:T(8,128)}, f32[128,128]{0,1:T(8,128)}) async-done(((f32[128,128]{0,1:T(8,128)}, f32[128,128]{0,1:T(8,128)}), (f32[128,128]{0,1:T(8,128)}, f32[128,128]{0,1:T(8,128)})) %all-reduce.3.cloned.1.call-update) | async-done | bytes 131088 | tf_op jit(solution)/shard_map/psum | solution.py:120
  (58 shorter events, 20.5 us)
Async XLA Ops:
  7.2 187.9 %copy-start = (f32[128,128]{1,0:T(8,128)S(1)}, f32[128,128]{1,0:T(8,128)}, u32[]{:S(2)}) copy-start(f32[128,128]{1,0:T(8,128)} %param.20) | copy-start | bytes 196612
  7.2 187.9 %all-gather.3.cloned.1.call-start = ((), (), s32[]{:S(2)}) async-start(), calls=%async_computation.2 | async-start | bytes 8912896 | tf_op jit(solution)/shard_map/all_gather | solution.py:38
  7.9 354.7 %reduce-scatter.3.cloned.1.call-start = ((), (), s32[]{:S(2)}) async-start(), calls=%async_computation.3 | async-start | bytes 8912896 | tf_op jit(solution)/shard_map/reduce_scatter | solution.py:68
  251.1 111.4 %copy-start.3 = (f32[1024,128]{1,0:T(8,128)S(1)}, f32[1024,128]{1,0:T(8,128)}, u32[]{:S(2)}) copy-start(f32[1024,128]{1,0:T(8,128)} %param.15) | copy-start | bytes 1572868
  251.1 111.4 %copy-start.5 = (f32[1024,128]{1,0:T(8,128)S(1)}, f32[1024,128]{1,0:T(8,128)}, u32[]{:S(2)}) copy-start(f32[1024,128]{1,0:T(8,128)} %param.25) | copy-start | bytes 1572868
  251.1 111.4 %copy-start.7 = (f32[128,128]{1,0:T(8,128)S(1)}, f32[128,128]{1,0:T(8,128)}, u32[]{:S(2)}) copy-start(f32[128,128]{1,0:T(8,128)} %param.19) | copy-start | bytes 196612
  251.1 111.4 %copy-start.8 = (f32[1024]{0:T(1024)S(1)}, f32[1024]{0:T(1024)}, u32[]{:S(2)}) copy-start(f32[1024]{0:T(1024)} %param.17) | copy-start | bytes 12292
  251.2 174.0 %all-gather.5.cloned.1.call-start = ((), (), s32[]{:S(2)}) async-start(), calls=%async_computation.4 | async-start | bytes 4456448 | tf_op jit(solution)/shard_map/all_gather | solution.py:89
  365.5 277.5 %reduce-scatter.5.cloned.1.call-start = ((), (), s32[]{:S(2)}) async-start(), calls=%async_computation.5 | async-start | bytes 8912896 | tf_op jit(solution)/shard_map/reduce_scatter | solution.py:110
  462.4 1.0 copy-start.4
  462.4 1.2 copy-start.6
  462.4 1.4 copy-start.9
  462.4 180.5 %copy-start.1 = (f32[1024,128]{1,0:T(8,128)S(1)}, f32[1024,128]{1,0:T(8,128)}, u32[]{:S(2)}) copy-start(f32[1024,128]{1,0:T(8,128)} %param.16) | copy-start | bytes 1572868
  462.4 180.5 %copy-start.2 = (f32[1024]{0:T(1024)S(1)}, f32[1024]{0:T(1024)}, u32[]{:S(2)}) copy-start(f32[1024]{0:T(1024)} %param.18) | copy-start | bytes 12292
  462.5 430.6 %all-reduce.3.cloned.1.call-start = ((), (), s32[]{:S(2)}) async-start(), calls=%async_computation.6 | async-start | bytes 262144 | tf_op jit(solution)/shard_map/psum | solution.py:120
Sparse Core Ops, SparseCore 0:
  9.8 185.2 all-gather.2
  251.3 111.2 reduce-scatter.2
  365.9 59.2 all-gather.4
  462.6 180.3 reduce-scatter.4
  649.0 244.0 all-reduce.2
where the time goes:
time: 904 us; the launch traced here: 903 us
  waiting for transfers between devices  726 us (80%)
  matrix products  78.1 us (9%)
  local copies, waits for them, and re-layouts  44 us (5%)
  blocking collectives  37 us (4%)
  between operations  14.6 us (2%)
    psum x1, waiting for transfers between devices, body(): grad_msg, grad_self = lax.psum((local_msg, local_self), ('cg', 'vg'))  245 us
    reduce_scatter x1, waiting for transfers between devices, body(): lax.psum_scatter(backward_sum.reshape(col_blocks * TB, H), 'cg', scatter_...  176 us
    all_gather x1, waiting for transfers between devices, body(): lax.all_gather(var_embed, 'cg', axis=0, tiled=True)  147 us
    reduce_scatter x1, waiting for transfers between devices, body(): lax.psum_scatter(forward_sum.reshape(row_blocks * TB, H), 'vg', scatter_d...  110 us
    all_gather x1, waiting for transfers between devices, body(): lax.all_gather(grad_messages, 'vg', axis=0, tiled=True)  47.1 us
    all_gather x1, blocking collectives, body(): lax.all_gather(col_coef, 'cg', axis=0, tiled=True)  37 us
    dot_general x1, matrix products, body(): jnp.dot(gathered, msg_weight, precision=highest, preferred_element_type=j...  18.7 us
  transfers between devices with their start and end apart: 5, of which 5 were waited for; matrix products, arithmetic and copies ran while one was open for 2% of the time, Pallas kernels for 0%

commit v1 on v0

--- a/solution.py
+++ b/solution.py
@@ -117,7 +117,7 @@
     local_msg = jnp.dot(
         var_embed.T, grad_lin, precision=highest, preferred_element_type=jnp.float32
     )
-    grad_msg, grad_self = lax.psum((local_msg, local_self), ("cg", "vg"))
+    grad_msg, grad_self = lax.psum(lax.psum((local_msg, local_self), "cg"), "vg")
     return (con_update, grad_con, grad_var, grad_msg, grad_self)
 
 

time: 904 us -> 940 us (1.040)
  waiting for transfers between devices: 726 us -> 760 us
    psum x1 -> x2, waiting for transfers between devices: 245 us -> 277 us  [the longest x1 142 us: body(): lax.psum(lax.psum((local_msg, local_self), 'cg'), 'vg')]
  transfers between devices with their start and end apart: 5 -> 6, of which waited for: 5 -> 6; matrix products, arithmetic and copies ran while one was open for 2% -> 2% of each run, Pallas kernels for 0% -> 0%
where the time goes in v1:
time: 940 us; the launch traced here: 937 us
  waiting for transfers between devices  760 us (81%)
  matrix products  78.2 us (8%)
  local copies, waits for them, and re-layouts  43.9 us (5%)
  blocking collectives  37 us (4%)
  between operations  14.9 us (2%)
    reduce_scatter x1, waiting for transfers between devices, body(): lax.psum_scatter(backward_sum.reshape(col_blocks * TB, H), 'cg', scatter_...  177 us
    all_gather x1, waiting for transfers between devices, body(): lax.all_gather(var_embed, 'cg', axis=0, tiled=True)  147 us
    psum x1, waiting for transfers between devices, body(): lax.psum(lax.psum((local_msg, local_self), 'cg'), 'vg')  142 us
    psum x1, waiting for transfers between devices, body(): lax.psum((local_msg, local_self), 'cg')  136 us
    reduce_scatter x1, waiting for transfers between devices, body(): lax.psum_scatter(forward_sum.reshape(row_blocks * TB, H), 'vg', scatter_d...  110 us
    all_gather x1, waiting for transfers between devices, body(): lax.all_gather(grad_messages, 'vg', axis=0, tiled=True)  47.2 us
    all_gather x1, blocking collectives, body(): lax.all_gather(col_coef, 'cg', axis=0, tiled=True)  37 us
  transfers between devices with their start and end apart: 6, of which 6 were waited for; matrix products, arithmetic and copies ran while one was open for 2% of the time, Pallas kernels for 0%

profile of v1, /device:TPU:2, one launch (start us, length us, event | category | flops | bytes accessed | tf_op | source)
XLA Modules:
  0.0 937.2 jit_solution(16485644198049491168)
XLA Ops:
  11.3 37.0 %all_gather.10 = f32[16384]{0:T(1024)S(1)} all-gather(f32[1024]{0:T(1024)} %param.18), channel_id=1, replica_groups=mesh['cg'=16,'vg'=16] {'cg'}, dimensions={0}, use_global_device_ids=true | all-gather | bytes 69632 | tf_op jit(solution)/shard_map/all_gather | solution.py:39
  48.3 146.8 %all-gather.3.cloned.1.call-done = f32[16384,128]{1,0:T(8,128)} async-done(((f32[1024,128]{1,0:T(8,128)}), f32[16384,128]{1,0:T(8,128)}) %all-gather.3.cloned.1.call-update) | async-done | bytes 8388624 | tf_op jit(solution)/shard_map/all_gather | solution.py:38
  195.1 18.7 %fusion.30 = bf16[16384,128]{1,0:T(8,128)(2,1)} fusion(f32[16384,128]{1,0:T(8,128)} %all-gather.3.cloned.1.call-done, f32[128,128]{1,0:T(8,128)S(1)} %copy-done, f32[16384]{0:T(1024)S(1)} %all_gather.10), kind=kOutput, calls=%fused_computation.39 | convolution fusion | flops 3225419776 | bytes 12713984 | tf_op jit(solution)/shard_map/dot_general | solution.py:42
  213.7 30.1 %while.22 = (s32[]{:T(128)}, f32[32,65536]{1,0:T(8,128)}, s32[2,8]{1,0:T(2,128)S(1)}, bf16[2,8,512,512]{3,2,1,0:T(8,128)(2,1)}, s32[2,8]{1,0:T(2,128)S(1)}, /*in...) while((s32[]{:T(128)}, f32[32,65536]{1,0:T(8,128)}, s32[2,8]{1,0:T(2,128)S(1)}, ...), condition=%wide.region_1.2_spmd.clone, body=%wide.region_0.1_spmd.clone.sunk | while | flops 742393088 | bytes 28316484 | solution.py:63
  213.8 2.9 gather_fusion
  216.7 3.4 fusion.65
  220.2 7.6 convolution_add_fusion.6
  227.8 2.9 gather_fusion
  230.7 3.4 fusion.65
  234.2 9.7 %convolution_add_fusion.6 = f32[32,65536]{1,0:T(8,128)} fusion(f32[32,65536]{1,0:T(8,128)} %get-tuple-element.265, pred[]{:T(512)S(6)} %compare.6, f32[1,8,512,128]{3,2,1,0:T(8,128)S(1)} %fusion.65, s32[8]{0:T(128)S(1)} %fusion.66), kind=kOutput, calls=%fused_computation.4.clone.1 | convolution fusion | flops 205521152 | bytes 18874400 | tf_op jit(solution)/shard_map/while/body/eval_jaxpr/dot_general | solution.py:55
  243.9 7.3 reshape.96
  252.2 110.4 %reduce-scatter.3.cloned.1.call-done = f32[1024,128]{1,0:T(8,128)} async-done(((f32[16384,128]{1,0:T(8,128)}), f32[1024,128]{1,0:T(8,128)}) %reduce-scatter.3.cloned.1.call-update) | async-done | bytes 524304 | tf_op jit(solution)/shard_map/reduce_scatter | solution.py:68
  365.7 12.3 %copy.20 = bf16[1,1,16,512,512]{3,4,2,1,0:T(8,128)(2,1)} copy(bf16[1,1,16,512,512]{4,3,2,1,0:T(8,128)(2,1)} %bitcast.88) | data formatting | bytes 16777216 | tf_op args[9]
  378.0 47.2 %all-gather.5.cloned.1.call-done = bf16[16384,128]{1,0:T(8,128)(2,1)} async-done(((bf16[1024,128]{1,0:T(8,128)(2,1)}), bf16[16384,128]{1,0:T(8,128)(2,1)}) %all-gather.5.cloned.1.call-update) | async-done | bytes 4194320 | tf_op jit(solution)/shard_map/all_gather | solution.py:89
  425.2 30.0 %while.23 = (s32[]{:T(128)}, f32[32,65536]{1,0:T(8,128)}, s32[2,8]{1,0:T(2,128)S(1)}, bf16[2,8,512,512]{2,3,1,0:T(8,128)(2,1)}, s32[2,8]{1,0:T(2,128)S(1)}, /*in...) while((s32[]{:T(128)}, f32[32,65536]{1,0:T(8,128)}, s32[2,8]{1,0:T(2,128)S(1)}, ...), condition=%wide.region_4.5_spmd.clone, body=%wide.region_3.4_spmd.clone.sunk | while | flops 742393088 | bytes 28316484 | solution.py:105
  428.2 3.4 fusion.71
  431.6 7.5 convolution_add_fusion.7
  439.1 2.9 gather_fusion.1
  442.1 3.4 fusion.71
  445.5 9.6 %convolution_add_fusion.7 = f32[32,65536]{1,0:T(8,128)} fusion(f32[32,65536]{1,0:T(8,128)} %get-tuple-element.289, pred[]{:T(512)S(6)} %compare.7, f32[1,8,512,128]{3,2,1,0:T(8,128)S(1)} %fusion.71, s32[8]{0:T(128)S(1)} %fusion.72), kind=kOutput, calls=%fused_computation.21.clone.1 | convolution fusion | flops 205521152 | bytes 18874400 | tf_op jit(solution)/shard_map/while/body/eval_jaxpr/dot_general | solution.py:97
  455.2 7.4 reshape.98
  465.7 177.4 %reduce-scatter.5.cloned.1.call-done = f32[1024,128]{1,0:T(8,128)} async-done(((f32[16384,128]{1,0:T(8,128)}), f32[1024,128]{1,0:T(8,128)}) %reduce-scatter.5.cloned.1.call-update) | async-done | bytes 524304 | tf_op jit(solution)/shard_map/reduce_scatter | solution.py:110
  647.5 135.5 %all-reduce.7.cloned.1.call-done = (f32[128,128]{0,1:T(8,128)}, f32[128,128]{0,1:T(8,128)}) async-done(((f32[128,128]{0,1:T(8,128)}, f32[128,128]{0,1:T(8,128)}), (f32[128,128]{0,1:T(8,128)}, f32[128,128]{0,1:T(8,128)})) %all-reduce.7.cloned.1.call-update) | async-done | bytes 131088 | tf_op jit(solution)/shard_map/psum | solution.py:120
  785.5 141.7 %all-reduce.5.cloned.1.call-done = (f32[128,128]{0,1:T(8,128)}, f32[128,128]{0,1:T(8,128)}) async-done(((f32[128,128]{0,1:T(8,128)}, f32[128,128]{0,1:T(8,128)}), (f32[128,128]{0,1:T(8,128)}, f32[128,128]{0,1:T(8,128)})) %all-reduce.5.cloned.1.call-update) | async-done | bytes 131088 | tf_op jit(solution)/shard_map/psum | solution.py:120
  (61 shorter events, 23.5 us)
Async XLA Ops:
  7.2 187.9 %copy-start = (f32[128,128]{1,0:T(8,128)S(1)}, f32[128,128]{1,0:T(8,128)}, u32[]{:S(2)}) copy-start(f32[128,128]{1,0:T(8,128)} %param.20) | copy-start | bytes 196612
  7.2 187.9 %all-gather.3.cloned.1.call-start = ((), (), s32[]{:S(2)}) async-start(), calls=%async_computation.2 | async-start | bytes 8912896 | tf_op jit(solution)/shard_map/all_gather | solution.py:38
  7.9 354.7 %reduce-scatter.3.cloned.1.call-start = ((), (), s32[]{:S(2)}) async-start(), calls=%async_computation.3 | async-start | bytes 8912896 | tf_op jit(solution)/shard_map/reduce_scatter | solution.py:68
  251.2 111.4 %copy-start.3 = (f32[1024,128]{1,0:T(8,128)S(1)}, f32[1024,128]{1,0:T(8,128)}, u32[]{:S(2)}) copy-start(f32[1024,128]{1,0:T(8,128)} %param.15) | copy-start | bytes 1572868
  251.2 111.4 %copy-start.5 = (f32[1024,128]{1,0:T(8,128)S(1)}, f32[1024,128]{1,0:T(8,128)}, u32[]{:S(2)}) copy-start(f32[1024,128]{1,0:T(8,128)} %param.25) | copy-start | bytes 1572868
  251.2 111.4 %copy-start.7 = (f32[128,128]{1,0:T(8,128)S(1)}, f32[128,128]{1,0:T(8,128)}, u32[]{:S(2)}) copy-start(f32[128,128]{1,0:T(8,128)} %param.19) | copy-start | bytes 196612
  251.2 111.4 %copy-start.8 = (f32[1024]{0:T(1024)S(1)}, f32[1024]{0:T(1024)}, u32[]{:S(2)}) copy-start(f32[1024]{0:T(1024)} %param.17) | copy-start | bytes 12292
  251.2 173.9 %all-gather.5.cloned.1.call-start = ((), (), s32[]{:S(2)}) async-start(), calls=%async_computation.4 | async-start | bytes 4456448 | tf_op jit(solution)/shard_map/all_gather | solution.py:89
  365.5 277.6 %reduce-scatter.5.cloned.1.call-start = ((), (), s32[]{:S(2)}) async-start(), calls=%async_computation.5 | async-start | bytes 8912896 | tf_op jit(solution)/shard_map/reduce_scatter | solution.py:110
  462.6 1.0 copy-start.4
  462.6 1.2 copy-start.6
  462.6 1.4 copy-start.9
  462.6 180.5 %copy-start.1 = (f32[1024,128]{1,0:T(8,128)S(1)}, f32[1024,128]{1,0:T(8,128)}, u32[]{:S(2)}) copy-start(f32[1024,128]{1,0:T(8,128)} %param.16) | copy-start | bytes 1572868
  462.6 180.5 %copy-start.2 = (f32[1024]{0:T(1024)S(1)}, f32[1024]{0:T(1024)}, u32[]{:S(2)}) copy-start(f32[1024]{0:T(1024)} %param.18) | copy-start | bytes 12292
  462.6 320.4 %all-reduce.7.cloned.1.call-start = ((), (), s32[]{:S(2)}) async-start(), calls=%async_computation.7 | async-start | bytes 262144 | tf_op jit(solution)/shard_map/psum | solution.py:120
  646.0 281.3 %all-reduce.5.cloned.1.call-start = ((), (), s32[]{:S(2)}) async-start(), calls=%async_computation.6 | async-start | bytes 262144 | tf_op jit(solution)/shard_map/psum | solution.py:120
Sparse Core Ops, SparseCore 0:
  9.8 185.2 all-gather.2
  251.4 111.1 reduce-scatter.2
  365.9 59.2 all-gather.4
  462.7 180.3 reduce-scatter.4
  646.2 136.8 all-reduce.6
  785.7 141.4 all-reduce.4
